TPU v7x, 256 devices: a whole 4x4x8 slice. The times are simulated.
256 devices in a mesh: row: 8 (over z), col: 32 (over x, y, core).
Axes of the slice: x: 4, y: 4, z: 8, core: 2. Of those that a mesh axis runs over, the one named last changes fastest.
Arguments:
- inputs: bfloat16 [1024, 16, 1024], P('col', 'row'), may hold values from -6 to 6
- weight: bfloat16 [1024, 27, 1024], P('col', None, 'row'), may hold values from -0.0390625 to 0.0390625
- grad_out: bfloat16 [1024, 16, 1024], P('col', 'row'), may hold values from -6 to 6
Outputs:
- outputs: bfloat16 [1024, 16, 1024], P('col', 'row')
- grad_in: bfloat16 [1024, 16, 1024], P('col', 'row')
- grad_weight: float32 [1024, 27, 1024], P('col', None, 'row')
All inputs are finite; a program needn't handle non-finite values.
Results may differ from a plain program's by a relative error of at most 0.0011.
Values may be sent and summed in bfloat16 or wider, within the bound.
A program may use at most 128 MiB of HBM per device.

v0:
```python
import math

import jax
import jax.numpy as jnp
from jax import lax
from jax.sharding import PartitionSpec as P

BX = 32
BY = 32


kernel_offsets = [(a, b, e) for a in (-1, 0, 1) for b in (-1, 0, 1) for e in (-1, 0, 1)]


def extended(block, sides, width):
    for axis, dim in sides:
        count = lax.axis_size(axis)
        forward = [(i, i + 1) for i in range(count - 1)]
        backward = [(target, source) for source, target in forward]
        low = lax.ppermute(
            lax.slice_in_dim(block, block.shape[dim] - width, None, axis=dim), axis, forward
        )
        high = lax.ppermute(lax.slice_in_dim(block, 0, width, axis=dim), axis, backward)
        block = jnp.concatenate([low, block, high], axis=dim)
    return block


def plane_valid(shift_y, shift_x, extent):
    positions = jnp.arange(extent, dtype=jnp.int32) % (BY * BX)
    along_y = positions // BX + shift_y
    along_x = positions % BX + shift_x
    return (along_y >= 0) & (along_y < BY) & (along_x >= 0) & (along_x < BX)


def flat_rim(field):
    flattened = field.reshape(field.shape[0], -1)
    return jnp.pad(flattened, ((0, 0), (BX + 1, BX + 1)))


def shifted(flattened, planes, shift_z, shift_y, shift_x):
    extent = planes * BY * BX
    offset = BX + 1 + (1 + shift_z) * BY * BX + shift_y * BX + shift_x
    window = lax.slice_in_dim(flattened, offset, offset + extent, axis=1)
    return jnp.where(plane_valid(shift_y, shift_x, extent)[None, :], window, jnp.zeros_like(window))


def forward_columns(padded, planes):
    windows = [shifted(padded, planes, sz, sy, sx) for sz, sy, sx in kernel_offsets]
    stacked = jnp.stack(windows, axis=0)
    return stacked.reshape(27 * padded.shape[0], stacked.shape[2])


def backward_columns(padded, planes):
    windows = [shifted(padded, planes, -sz, -sy, -sx) for sz, sy, sx in kernel_offsets]
    stacked = jnp.stack(windows, axis=1)
    return stacked.reshape(padded.shape[0] * 27, stacked.shape[2])


def group_count(shard_count, unit):
    target = max(1, 128 // unit)
    best = 1
    for candidate in range(1, shard_count + 1):
        if shard_count % candidate == 0 and candidate <= target:
            best = candidate
    return best


def on_device(inputs, weight, grad_out):
    width_dev = inputs.shape[0]
    planes = inputs.shape[1]
    extent = planes * BY * BX
    gathered_weight = lax.all_gather(weight, "row", axis=2, tiled=True)
    out_width = gathered_weight.shape[0]
    channels = gathered_weight.shape[2]
    input_rim = extended(inputs, (("row", 1),), 1)
    grad_rim = extended(grad_out, (("row", 1),), 1)
    grad_rows = grad_out.reshape(out_width, extent)
    initial = (
        jnp.zeros((out_width, extent), jnp.float32),
        jnp.zeros((channels, 27 * out_width), jnp.float32),
    )
    shard_rows = lax.all_gather(input_rim, "col", axis=0, tiled=True)
    shard_count = shard_rows.shape[0] // width_dev
    group = group_count(shard_count, width_dev)
    block_rows = group * width_dev
    count_blocks = shard_count // group

    def one_block(b, state):
        output_sum, weight_sum = state
        first_channel = b * block_rows
        channel_block = lax.dynamic_slice_in_dim(shard_rows, b * block_rows, block_rows, 0)
        columns = forward_columns(flat_rim(channel_block), planes)
        weight_block = lax.dynamic_slice_in_dim(gathered_weight, first_channel, block_rows, 2)
        flat_weight = weight_block.reshape(out_width, 27 * block_rows)
        output_sum = output_sum + jnp.dot(flat_weight, columns, preferred_element_type=jnp.float32)
        block_grad = lax.dot_general(
            columns, grad_rows, (((1,), (1,)), ((), ())), preferred_element_type=jnp.float32
        )
        block_grad = block_grad.reshape(27, block_rows, out_width).transpose(1, 0, 2)
        block_grad = block_grad.reshape(block_rows, 27 * out_width)
        weight_sum = lax.dynamic_update_slice_in_dim(weight_sum, block_grad, first_channel, 0)
        return (output_sum, weight_sum)

    output_sum, weight_rows_sum = lax.fori_loop(0, count_blocks, one_block, initial)
    outputs = output_sum.astype(jnp.bfloat16).reshape(out_width, planes, BY * BX)
    weight_sum = weight_rows_sum.reshape(channels, 27, out_width).transpose(2, 1, 0)
    scale = 1.0 / math.sqrt(planes * lax.axis_size("row") * BY * BX)
    grad_weight = lax.psum_scatter(weight_sum, "row", scatter_dimension=2, tiled=True) * scale
    grad_columns = backward_columns(flat_rim(grad_rim), planes)
    flat_cols = gathered_weight.reshape(out_width * 27, width_dev * lax.axis_size("col"))
    grad_sum = lax.psum_scatter(
        lax.dot_general(
            flat_cols, grad_columns, (((0,), (0,)), ((), ())), preferred_element_type=jnp.float32
        ),
        "col",
        scatter_dimension=0,
        tiled=True,
    )
    grad_in = grad_sum.astype(jnp.bfloat16).reshape(width_dev, planes, BY * BX)
    return (outputs, grad_in, grad_weight)


def solution(mesh):
    placed = (P("col", "row", None), P("col", None, "row"), P("col", "row", None))
    return jax.shard_map(
        on_device,
        mesh=mesh,
        in_specs=placed,
        out_specs=(P("col", "row", None), P("col", "row", None), P("col", None, "row")),
        check_vma=False,
    )
```

profile of v0, /device:TPU:8, one launch (start us, length us, event | category | flops | bytes accessed | tf_op | source)
XLA Modules:
  0.0 398.2 jit_solution(570935348018330792)
XLA Ops:
  10.5 4.6 %collective-permute-start = (bf16[32,1,1024]{2,1,0:T(2,128)(2,1)S(1)}, bf16[32,1,1024]{2,1,0:T(2,128)(2,1)S(1)}, u32[]{:S(2)}, u32[]{:S(2)}) collective-permute-start(bf16[32,1,1024]{2,1,0:T(2,128)(2,1)S(1)} %get-tuple-element.234), channel_id=1, source_target_pairs={{0,32},{32,64},{64,96},{96,128},{128,160},{160,192},{192,224},{1,3... | collective-permute-start | bytes 196616 | tf_op jit(solution)/shard_map/ppermute | solution.py:20
  22.3 5.0 %collective-permute-start.2 = (bf16[32,1,1024]{2,1,0:T(2,128)(2,1)S(1)}, bf16[32,1,1024]{2,1,0:T(2,128)(2,1)S(1)}, u32[]{:S(2)}, u32[]{:S(2)}) collective-permute-start(bf16[32,1,1024]{2,1,0:T(2,128)(2,1)S(1)} %get-tuple-element.232), channel_id=1, source_target_pairs={{0,32},{32,64},{64,96},{96,128},{128,160},{160,192},{192,224},{1,3... | collective-permute-start | bytes 196616 | tf_op jit(solution)/shard_map/ppermute | solution.py:20
  34.5 24.3 %all-gather.3.cloned.1.call-done = bf16[32,27,1024]{2,0,1:T(8,128)(2,1)} async-done(((bf16[32,27,128]{2,0,1:T(8,128)(2,1)}), bf16[32,27,1024]{2,0,1:T(8,128)(2,1)}) %all-gather.3.cloned.1.call-update) | async-done | bytes 1769488 | tf_op jit(solution)/shard_map/all_gather | solution.py:72
  58.9 8.2 %convolution_bitcast_fusion.1 = f32[1024,2048]{0,1:T(8,128)} fusion(bf16[32,27,2048]{2,0,1:T(8,128)(2,1)S(1)} %bitcast_dynamic-update-slice_fusion.8, bf16[32,27,1024]{2,0,1:T(8,128)(2,1)} %all-gather.3.cloned.1.call-done), kind=kOutput, calls=%fused_computation.105 | convolution fusion | flops 3623878656 | bytes 13697024 | tf_op jit(solution)/shard_map/dot_general | solution.py:112
  67.1 9.2 %copy.8 = f32[1024,2048]{1,0:T(8,128)} copy(f32[1024,2048]{0,1:T(8,128)} %convolution_bitcast_fusion.1) | data formatting | bytes 16777216
  76.3 42.7 %all-gather.5.cloned.1.call-done = bf16[1024,4,1024]{2,1,0:T(4,128)(2,1)} async-done(((bf16[32,4,1024]{2,1,0:T(4,128)(2,1)}), bf16[1024,4,1024]{2,1,0:T(4,128)(2,1)}) %all-gather.5.cloned.1.call-update) | async-done | bytes 8388624 | tf_op jit(solution)/shard_map/all_gather | solution.py:82
  119.4 219.4 %while.19 = (s32[]{:T(128)}, f32[32,2048]{1,0:T(8,128)}, f32[1024,864]{0,1:T(8,128)S(1)}, bf16[32,27,1024]{2,0,1:T(8,128)(2,1)}, bf16[1024,4,1024]{2,1,0:T(4,128...) while((s32[]{:T(128)}, f32[32,2048]{1,0:T(8,128)}, ...), condition=%wide.region_1.2_spmd.clone, body=%wide.region_0.1_spmd.clone.sunk | while | flops 913793024 | bytes 181059872 | solution.py:104
  127.9 5.0 %copy-done = bf16[27,128,2048]{2,1,0:T(8,128)(2,1)} copy-done((bf16[27,128,2048]{2,1,0:T(8,128)(2,1)}, bf16[27,128,2048]{2,1,0:T(8,128)(2,1)S(1)}, u32[]{:S(2)}) %copy-start) | copy-done | bytes 14155800 | tf_op jit(solution)/shard_map/while
  133.0 9.1 %fusion.147 = f32[32,2048]{1,0:T(8,128)} fusion(bf16[27,128,2048]{2,1,0:T(8,128)(2,1)} %copy-done, f32[32,2048]{1,0:T(8,128)} %get-tuple-element.284, bf16[32,27,1024]{2,0,1:T(8,128)(2,1)} %get-tuple-element.296, s32[]{:T(128)S(6)} %select_n.2038, pred[]{:T(512)S(6)} %compare.180), kind=kOutput, calls=%fused_computation.1.clone.1 | convolution fusion | flops 453115904 | bytes 14901253 | tf_op jit(solution)/shard_map/while/body/eval_jaxpr/dot_general | solution.py:95
  143.6 4.3 %fusion.148 = f32[27,128,32]{1,2,0:T(8,128)S(1)} fusion(bf16[27,128,2048]{2,1,0:T(8,128)(2,1)S(1)} %copy-done.1, bf16[32,2048]{1,0:T(8,128)(2,1)S(1)} %copy-done.3), kind=kOutput, calls=%fused_computation.68.clone.1 | convolution fusion | flops 452984832 | bytes 14729216 | tf_op jit(solution)/shard_map/while/body/eval_jaxpr/dot_general | solution.py:96
  156.3 5.5 %copy-done = bf16[27,128,2048]{2,1,0:T(8,128)(2,1)} copy-done((bf16[27,128,2048]{2,1,0:T(8,128)(2,1)}, bf16[27,128,2048]{2,1,0:T(8,128)(2,1)S(1)}, u32[]{:S(2)}) %copy-start) | copy-done | bytes 14155800 | tf_op jit(solution)/shard_map/while
  161.8 8.8 %fusion.147 = f32[32,2048]{1,0:T(8,128)} fusion(bf16[27,128,2048]{2,1,0:T(8,128)(2,1)} %copy-done, f32[32,2048]{1,0:T(8,128)} %get-tuple-element.284, bf16[32,27,1024]{2,0,1:T(8,128)(2,1)} %get-tuple-element.296, s32[]{:T(128)S(6)} %select_n.2038, pred[]{:T(512)S(6)} %compare.180), kind=kOutput, calls=%fused_computation.1.clone.1 | convolution fusion | flops 453115904 | bytes 14901253 | tf_op jit(solution)/shard_map/while/body/eval_jaxpr/dot_general | solution.py:95
  171.4 4.3 %fusion.148 = f32[27,128,32]{1,2,0:T(8,128)S(1)} fusion(bf16[27,128,2048]{2,1,0:T(8,128)(2,1)S(1)} %copy-done.1, bf16[32,2048]{1,0:T(8,128)(2,1)S(1)} %copy-done.3), kind=kOutput, calls=%fused_computation.68.clone.1 | convolution fusion | flops 452984832 | bytes 14729216 | tf_op jit(solution)/shard_map/while/body/eval_jaxpr/dot_general | solution.py:96
  184.1 5.0 %copy-done = bf16[27,128,2048]{2,1,0:T(8,128)(2,1)} copy-done((bf16[27,128,2048]{2,1,0:T(8,128)(2,1)}, bf16[27,128,2048]{2,1,0:T(8,128)(2,1)S(1)}, u32[]{:S(2)}) %copy-start) | copy-done | bytes 14155800 | tf_op jit(solution)/shard_map/while
  189.1 8.8 %fusion.147 = f32[32,2048]{1,0:T(8,128)} fusion(bf16[27,128,2048]{2,1,0:T(8,128)(2,1)} %copy-done, f32[32,2048]{1,0:T(8,128)} %get-tuple-element.284, bf16[32,27,1024]{2,0,1:T(8,128)(2,1)} %get-tuple-element.296, s32[]{:T(128)S(6)} %select_n.2038, pred[]{:T(512)S(6)} %compare.180), kind=kOutput, calls=%fused_computation.1.clone.1 | convolution fusion | flops 453115904 | bytes 14901253 | tf_op jit(solution)/shard_map/while/body/eval_jaxpr/dot_general | solution.py:95
  199.0 4.3 %fusion.148 = f32[27,128,32]{1,2,0:T(8,128)S(1)} fusion(bf16[27,128,2048]{2,1,0:T(8,128)(2,1)S(1)} %copy-done.1, bf16[32,2048]{1,0:T(8,128)(2,1)S(1)} %copy-done.3), kind=kOutput, calls=%fused_computation.68.clone.1 | convolution fusion | flops 452984832 | bytes 14729216 | tf_op jit(solution)/shard_map/while/body/eval_jaxpr/dot_general | solution.py:96
  211.7 5.0 %copy-done = bf16[27,128,2048]{2,1,0:T(8,128)(2,1)} copy-done((bf16[27,128,2048]{2,1,0:T(8,128)(2,1)}, bf16[27,128,2048]{2,1,0:T(8,128)(2,1)S(1)}, u32[]{:S(2)}) %copy-start) | copy-done | bytes 14155800 | tf_op jit(solution)/shard_map/while
  216.7 8.6 %fusion.147 = f32[32,2048]{1,0:T(8,128)} fusion(bf16[27,128,2048]{2,1,0:T(8,128)(2,1)} %copy-done, f32[32,2048]{1,0:T(8,128)} %get-tuple-element.284, bf16[32,27,1024]{2,0,1:T(8,128)(2,1)} %get-tuple-element.296, s32[]{:T(128)S(6)} %select_n.2038, pred[]{:T(512)S(6)} %compare.180), kind=kOutput, calls=%fused_computation.1.clone.1 | convolution fusion | flops 453115904 | bytes 14901253 | tf_op jit(solution)/shard_map/while/body/eval_jaxpr/dot_general | solution.py:95
  226.3 4.3 %fusion.148 = f32[27,128,32]{1,2,0:T(8,128)S(1)} fusion(bf16[27,128,2048]{2,1,0:T(8,128)(2,1)S(1)} %copy-done.1, bf16[32,2048]{1,0:T(8,128)(2,1)S(1)} %copy-done.3), kind=kOutput, calls=%fused_computation.68.clone.1 | convolution fusion | flops 452984832 | bytes 14729216 | tf_op jit(solution)/shard_map/while/body/eval_jaxpr/dot_general | solution.py:96
  238.9 5.0 %copy-done = bf16[27,128,2048]{2,1,0:T(8,128)(2,1)} copy-done((bf16[27,128,2048]{2,1,0:T(8,128)(2,1)}, bf16[27,128,2048]{2,1,0:T(8,128)(2,1)S(1)}, u32[]{:S(2)}) %copy-start) | copy-done | bytes 14155800 | tf_op jit(solution)/shard_map/while
  244.0 8.5 %fusion.147 = f32[32,2048]{1,0:T(8,128)} fusion(bf16[27,128,2048]{2,1,0:T(8,128)(2,1)} %copy-done, f32[32,2048]{1,0:T(8,128)} %get-tuple-element.284, bf16[32,27,1024]{2,0,1:T(8,128)(2,1)} %get-tuple-element.296, s32[]{:T(128)S(6)} %select_n.2038, pred[]{:T(512)S(6)} %compare.180), kind=kOutput, calls=%fused_computation.1.clone.1 | convolution fusion | flops 453115904 | bytes 14901253 | tf_op jit(solution)/shard_map/while/body/eval_jaxpr/dot_general | solution.py:95
  253.3 4.3 %fusion.148 = f32[27,128,32]{1,2,0:T(8,128)S(1)} fusion(bf16[27,128,2048]{2,1,0:T(8,128)(2,1)S(1)} %copy-done.1, bf16[32,2048]{1,0:T(8,128)(2,1)S(1)} %copy-done.3), kind=kOutput, calls=%fused_computation.68.clone.1 | convolution fusion | flops 452984832 | bytes 14729216 | tf_op jit(solution)/shard_map/while/body/eval_jaxpr/dot_general | solution.py:96
  266.0 5.0 %copy-done = bf16[27,128,2048]{2,1,0:T(8,128)(2,1)} copy-done((bf16[27,128,2048]{2,1,0:T(8,128)(2,1)}, bf16[27,128,2048]{2,1,0:T(8,128)(2,1)S(1)}, u32[]{:S(2)}) %copy-start) | copy-done | bytes 14155800 | tf_op jit(solution)/shard_map/while
  271.0 8.5 %fusion.147 = f32[32,2048]{1,0:T(8,128)} fusion(bf16[27,128,2048]{2,1,0:T(8,128)(2,1)} %copy-done, f32[32,2048]{1,0:T(8,128)} %get-tuple-element.284, bf16[32,27,1024]{2,0,1:T(8,128)(2,1)} %get-tuple-element.296, s32[]{:T(128)S(6)} %select_n.2038, pred[]{:T(512)S(6)} %compare.180), kind=kOutput, calls=%fused_computation.1.clone.1 | convolution fusion | flops 453115904 | bytes 14901253 | tf_op jit(solution)/shard_map/while/body/eval_jaxpr/dot_general | solution.py:95
  280.4 4.3 %fusion.148 = f32[27,128,32]{1,2,0:T(8,128)S(1)} fusion(bf16[27,128,2048]{2,1,0:T(8,128)(2,1)S(1)} %copy-done.1, bf16[32,2048]{1,0:T(8,128)(2,1)S(1)} %copy-done.3), kind=kOutput, calls=%fused_computation.68.clone.1 | convolution fusion | flops 452984832 | bytes 14729216 | tf_op jit(solution)/shard_map/while/body/eval_jaxpr/dot_general | solution.py:96
  293.1 5.0 %copy-done = bf16[27,128,2048]{2,1,0:T(8,128)(2,1)} copy-done((bf16[27,128,2048]{2,1,0:T(8,128)(2,1)}, bf16[27,128,2048]{2,1,0:T(8,128)(2,1)S(1)}, u32[]{:S(2)}) %copy-start) | copy-done | bytes 14155800 | tf_op jit(solution)/shard_map/while
  298.1 8.5 %fusion.147 = f32[32,2048]{1,0:T(8,128)} fusion(bf16[27,128,2048]{2,1,0:T(8,128)(2,1)} %copy-done, f32[32,2048]{1,0:T(8,128)} %get-tuple-element.284, bf16[32,27,1024]{2,0,1:T(8,128)(2,1)} %get-tuple-element.296, s32[]{:T(128)S(6)} %select_n.2038, pred[]{:T(512)S(6)} %compare.180), kind=kOutput, calls=%fused_computation.1.clone.1 | convolution fusion | flops 453115904 | bytes 14901253 | tf_op jit(solution)/shard_map/while/body/eval_jaxpr/dot_general | solution.py:95
  307.4 4.3 %fusion.148 = f32[27,128,32]{1,2,0:T(8,128)S(1)} fusion(bf16[27,128,2048]{2,1,0:T(8,128)(2,1)S(1)} %copy-done.1, bf16[32,2048]{1,0:T(8,128)(2,1)S(1)} %copy-done.3), kind=kOutput, calls=%fused_computation.68.clone.1 | convolution fusion | flops 452984832 | bytes 14729216 | tf_op jit(solution)/shard_map/while/body/eval_jaxpr/dot_general | solution.py:96
  320.1 5.0 %copy-done = bf16[27,128,2048]{2,1,0:T(8,128)(2,1)} copy-done((bf16[27,128,2048]{2,1,0:T(8,128)(2,1)}, bf16[27,128,2048]{2,1,0:T(8,128)(2,1)S(1)}, u32[]{:S(2)}) %copy-start) | copy-done | bytes 14155800 | tf_op jit(solution)/shard_map/while
  325.2 8.5 %fusion.147 = f32[32,2048]{1,0:T(8,128)} fusion(bf16[27,128,2048]{2,1,0:T(8,128)(2,1)} %copy-done, f32[32,2048]{1,0:T(8,128)} %get-tuple-element.284, bf16[32,27,1024]{2,0,1:T(8,128)(2,1)} %get-tuple-element.296, s32[]{:T(128)S(6)} %select_n.2038, pred[]{:T(512)S(6)} %compare.180), kind=kOutput, calls=%fused_computation.1.clone.1 | convolution fusion | flops 453115904 | bytes 14901253 | tf_op jit(solution)/shard_map/while/body/eval_jaxpr/dot_general | solution.py:95
  334.5 4.3 %fusion.148 = f32[27,128,32]{1,2,0:T(8,128)S(1)} fusion(bf16[27,128,2048]{2,1,0:T(8,128)(2,1)S(1)} %copy-done.1, bf16[32,2048]{1,0:T(8,128)(2,1)S(1)} %copy-done.3), kind=kOutput, calls=%fused_computation.68.clone.1 | convolution fusion | flops 452984832 | bytes 14729216 | tf_op jit(solution)/shard_map/while/body/eval_jaxpr/dot_general | solution.py:96
  344.5 45.4 %reduce-scatter.5.cloned.1.call-done = f32[32,27,128]{2,0,1:T(8,128)} async-done(((f32[32,27,1024]{2,0,1:T(8,128)}), f32[32,27,128]{2,0,1:T(8,128)}) %reduce-scatter.5.cloned.1.call-update) | async-done | bytes 442384 | tf_op jit(solution)/shard_map/reduce_scatter | solution.py:108
  (418 shorter events, 97.4 us)
Async XLA Ops:
  7.2 51.7 %all-gather.3.cloned.1.call-start = ((), (), s32[]{:S(2)}) async-start(), calls=%async_computation.2 | async-start | bytes 1990656 | tf_op jit(solution)/shard_map/all_gather | solution.py:72
  7.9 111.1 %all-gather.5.cloned.1.call-start = ((), (), s32[]{:S(2)}) async-start(), calls=%async_computation.3 | async-start | bytes 8650752 | tf_op jit(solution)/shard_map/all_gather | solution.py:82
  9.2 7.3 %collective-permute-start.1 = (bf16[32,1,1024]{2,1,0:T(2,128)(2,1)S(1)}, bf16[32,1,1024]{2,1,0:T(2,128)(2,1)S(1)}, u32[]{:S(2)}, u32[]{:S(2)}) collective-permute-start(bf16[32,1,1024]{2,1,0:T(2,128)(2,1)S(1)} %get-tuple-element.235), channel_id=1, source_target_pairs={{32,0},{64,32},{96,64},{128,96},{160,128},{192,160},{224,192},{33,... | collective-permute-start | bytes 196616 | tf_op jit(solution)/shard_map/ppermute | solution.py:23
  10.5 7.2 %collective-permute-start = (bf16[32,1,1024]{2,1,0:T(2,128)(2,1)S(1)}, bf16[32,1,1024]{2,1,0:T(2,128)(2,1)S(1)}, u32[]{:S(2)}, u32[]{:S(2)}) collective-permute-start(bf16[32,1,1024]{2,1,0:T(2,128)(2,1)S(1)} %get-tuple-element.234), channel_id=1, source_target_pairs={{0,32},{32,64},{64,96},{96,128},{128,160},{160,192},{192,224},{1,3... | collective-permute-start | bytes 196616 | tf_op jit(solution)/shard_map/ppermute | solution.py:20
  19.8 320.9 %reduce-scatter.7.cloned.1.call-start = ((), (), s32[]{:S(2)}) async-start(), calls=%async_computation.5 | async-start | bytes 8650752
  21.0 9.3 %collective-permute-start.3 = (bf16[32,1,1024]{2,1,0:T(2,128)(2,1)S(1)}, bf16[32,1,1024]{2,1,0:T(2,128)(2,1)S(1)}, u32[]{:S(2)}, u32[]{:S(2)}) collective-permute-start(bf16[32,1,1024]{2,1,0:T(2,128)(2,1)S(1)} %get-tuple-element.233), channel_id=1, source_target_pairs={{32,0},{64,32},{96,64},{128,96},{160,128},{192,160},{224,192},{33,... | collective-permute-start | bytes 196616 | tf_op jit(solution)/shard_map/ppermute | solution.py:23
  22.3 8.0 %collective-permute-start.2 = (bf16[32,1,1024]{2,1,0:T(2,128)(2,1)S(1)}, bf16[32,1,1024]{2,1,0:T(2,128)(2,1)S(1)}, u32[]{:S(2)}, u32[]{:S(2)}) collective-permute-start(bf16[32,1,1024]{2,1,0:T(2,128)(2,1)S(1)} %get-tuple-element.232), channel_id=1, source_target_pairs={{0,32},{32,64},{64,96},{96,128},{128,160},{160,192},{192,224},{1,3... | collective-permute-start | bytes 196616 | tf_op jit(solution)/shard_map/ppermute | solution.py:20
  76.3 313.6 %reduce-scatter.5.cloned.1.call-start = ((), (), s32[]{:S(2)}) async-start(), calls=%async_computation.4 | async-start | bytes 3981312 | tf_op jit(solution)/shard_map/reduce_scatter | solution.py:108
  127.9 5.1 %copy-start = (bf16[27,128,2048]{2,1,0:T(8,128)(2,1)}, bf16[27,128,2048]{2,1,0:T(8,128)(2,1)S(1)}, u32[]{:S(2)}) copy-start(bf16[27,128,2048]{2,1,0:T(8,128)(2,1)S(1)} %bitcast_dynamic-update-slice_fusion.31) | copy-start | bytes 42467332 | tf_op jit(solution)/shard_map/while
  133.0 10.6 %copy-start.1 = (bf16[27,128,2048]{2,1,0:T(8,128)(2,1)S(1)}, bf16[27,128,2048]{2,1,0:T(8,128)(2,1)}, u32[]{:S(2)}) copy-start(bf16[27,128,2048]{2,1,0:T(8,128)(2,1)} %copy-done) | copy-start | bytes 42467332 | tf_op jit(solution)/shard_map/while
  133.0 10.6 %copy-start.3 = (bf16[32,2048]{1,0:T(8,128)(2,1)S(1)}, bf16[32,2048]{1,0:T(8,128)(2,1)}, u32[]{:S(2)}) copy-start(bf16[32,2048]{1,0:T(8,128)(2,1)} %get-tuple-element.298) | copy-start | bytes 393220 | tf_op jit(solution)/shard_map/while
  156.3 5.5 %copy-start = (bf16[27,128,2048]{2,1,0:T(8,128)(2,1)}, bf16[27,128,2048]{2,1,0:T(8,128)(2,1)S(1)}, u32[]{:S(2)}) copy-start(bf16[27,128,2048]{2,1,0:T(8,128)(2,1)S(1)} %bitcast_dynamic-update-slice_fusion.31) | copy-start | bytes 42467332 | tf_op jit(solution)/shard_map/while
  161.8 9.6 %copy-start.1 = (bf16[27,128,2048]{2,1,0:T(8,128)(2,1)S(1)}, bf16[27,128,2048]{2,1,0:T(8,128)(2,1)}, u32[]{:S(2)}) copy-start(bf16[27,128,2048]{2,1,0:T(8,128)(2,1)} %copy-done) | copy-start | bytes 42467332 | tf_op jit(solution)/shard_map/while
  161.8 9.6 %copy-start.3 = (bf16[32,2048]{1,0:T(8,128)(2,1)S(1)}, bf16[32,2048]{1,0:T(8,128)(2,1)}, u32[]{:S(2)}) copy-start(bf16[32,2048]{1,0:T(8,128)(2,1)} %get-tuple-element.298) | copy-start | bytes 393220 | tf_op jit(solution)/shard_map/while
  184.1 5.1 %copy-start = (bf16[27,128,2048]{2,1,0:T(8,128)(2,1)}, bf16[27,128,2048]{2,1,0:T(8,128)(2,1)S(1)}, u32[]{:S(2)}) copy-start(bf16[27,128,2048]{2,1,0:T(8,128)(2,1)S(1)} %bitcast_dynamic-update-slice_fusion.31) | copy-start | bytes 42467332 | tf_op jit(solution)/shard_map/while
  189.1 9.9 %copy-start.1 = (bf16[27,128,2048]{2,1,0:T(8,128)(2,1)S(1)}, bf16[27,128,2048]{2,1,0:T(8,128)(2,1)}, u32[]{:S(2)}) copy-start(bf16[27,128,2048]{2,1,0:T(8,128)(2,1)} %copy-done) | copy-start | bytes 42467332 | tf_op jit(solution)/shard_map/while
  189.1 9.9 %copy-start.3 = (bf16[32,2048]{1,0:T(8,128)(2,1)S(1)}, bf16[32,2048]{1,0:T(8,128)(2,1)}, u32[]{:S(2)}) copy-start(bf16[32,2048]{1,0:T(8,128)(2,1)} %get-tuple-element.298) | copy-start | bytes 393220 | tf_op jit(solution)/shard_map/while
  211.7 5.1 %copy-start = (bf16[27,128,2048]{2,1,0:T(8,128)(2,1)}, bf16[27,128,2048]{2,1,0:T(8,128)(2,1)S(1)}, u32[]{:S(2)}) copy-start(bf16[27,128,2048]{2,1,0:T(8,128)(2,1)S(1)} %bitcast_dynamic-update-slice_fusion.31) | copy-start | bytes 42467332 | tf_op jit(solution)/shard_map/while
  216.7 9.5 %copy-start.1 = (bf16[27,128,2048]{2,1,0:T(8,128)(2,1)S(1)}, bf16[27,128,2048]{2,1,0:T(8,128)(2,1)}, u32[]{:S(2)}) copy-start(bf16[27,128,2048]{2,1,0:T(8,128)(2,1)} %copy-done) | copy-start | bytes 42467332 | tf_op jit(solution)/shard_map/while
  216.7 9.5 %copy-start.3 = (bf16[32,2048]{1,0:T(8,128)(2,1)S(1)}, bf16[32,2048]{1,0:T(8,128)(2,1)}, u32[]{:S(2)}) copy-start(bf16[32,2048]{1,0:T(8,128)(2,1)} %get-tuple-element.298) | copy-start | bytes 393220 | tf_op jit(solution)/shard_map/while
  238.9 5.1 %copy-start = (bf16[27,128,2048]{2,1,0:T(8,128)(2,1)}, bf16[27,128,2048]{2,1,0:T(8,128)(2,1)S(1)}, u32[]{:S(2)}) copy-start(bf16[27,128,2048]{2,1,0:T(8,128)(2,1)S(1)} %bitcast_dynamic-update-slice_fusion.31) | copy-start | bytes 42467332 | tf_op jit(solution)/shard_map/while
  244.0 9.3 %copy-start.1 = (bf16[27,128,2048]{2,1,0:T(8,128)(2,1)S(1)}, bf16[27,128,2048]{2,1,0:T(8,128)(2,1)}, u32[]{:S(2)}) copy-start(bf16[27,128,2048]{2,1,0:T(8,128)(2,1)} %copy-done) | copy-start | bytes 42467332 | tf_op jit(solution)/shard_map/while
  244.0 9.3 %copy-start.3 = (bf16[32,2048]{1,0:T(8,128)(2,1)S(1)}, bf16[32,2048]{1,0:T(8,128)(2,1)}, u32[]{:S(2)}) copy-start(bf16[32,2048]{1,0:T(8,128)(2,1)} %get-tuple-element.298) | copy-start | bytes 393220 | tf_op jit(solution)/shard_map/while
  266.0 5.1 %copy-start = (bf16[27,128,2048]{2,1,0:T(8,128)(2,1)}, bf16[27,128,2048]{2,1,0:T(8,128)(2,1)S(1)}, u32[]{:S(2)}) copy-start(bf16[27,128,2048]{2,1,0:T(8,128)(2,1)S(1)} %bitcast_dynamic-update-slice_fusion.31) | copy-start | bytes 42467332 | tf_op jit(solution)/shard_map/while
  271.0 9.3 %copy-start.1 = (bf16[27,128,2048]{2,1,0:T(8,128)(2,1)S(1)}, bf16[27,128,2048]{2,1,0:T(8,128)(2,1)}, u32[]{:S(2)}) copy-start(bf16[27,128,2048]{2,1,0:T(8,128)(2,1)} %copy-done) | copy-start | bytes 42467332 | tf_op jit(solution)/shard_map/while
  271.0 9.3 %copy-start.3 = (bf16[32,2048]{1,0:T(8,128)(2,1)S(1)}, bf16[32,2048]{1,0:T(8,128)(2,1)}, u32[]{:S(2)}) copy-start(bf16[32,2048]{1,0:T(8,128)(2,1)} %get-tuple-element.298) | copy-start | bytes 393220 | tf_op jit(solution)/shard_map/while
  293.0 5.1 %copy-start = (bf16[27,128,2048]{2,1,0:T(8,128)(2,1)}, bf16[27,128,2048]{2,1,0:T(8,128)(2,1)S(1)}, u32[]{:S(2)}) copy-start(bf16[27,128,2048]{2,1,0:T(8,128)(2,1)S(1)} %bitcast_dynamic-update-slice_fusion.31) | copy-start | bytes 42467332 | tf_op jit(solution)/shard_map/while
  298.1 9.3 %copy-start.1 = (bf16[27,128,2048]{2,1,0:T(8,128)(2,1)S(1)}, bf16[27,128,2048]{2,1,0:T(8,128)(2,1)}, u32[]{:S(2)}) copy-start(bf16[27,128,2048]{2,1,0:T(8,128)(2,1)} %copy-done) | copy-start | bytes 42467332 | tf_op jit(solution)/shard_map/while
  298.1 9.3 %copy-start.3 = (bf16[32,2048]{1,0:T(8,128)(2,1)S(1)}, bf16[32,2048]{1,0:T(8,128)(2,1)}, u32[]{:S(2)}) copy-start(bf16[32,2048]{1,0:T(8,128)(2,1)} %get-tuple-element.298) | copy-start | bytes 393220 | tf_op jit(solution)/shard_map/while
  320.1 5.1 %copy-start = (bf16[27,128,2048]{2,1,0:T(8,128)(2,1)}, bf16[27,128,2048]{2,1,0:T(8,128)(2,1)S(1)}, u32[]{:S(2)}) copy-start(bf16[27,128,2048]{2,1,0:T(8,128)(2,1)S(1)} %bitcast_dynamic-update-slice_fusion.31) | copy-start | bytes 42467332 | tf_op jit(solution)/shard_map/while
  325.2 9.3 %copy-start.1 = (bf16[27,128,2048]{2,1,0:T(8,128)(2,1)S(1)}, bf16[27,128,2048]{2,1,0:T(8,128)(2,1)}, u32[]{:S(2)}) copy-start(bf16[27,128,2048]{2,1,0:T(8,128)(2,1)} %copy-done) | copy-start | bytes 42467332 | tf_op jit(solution)/shard_map/while
  325.2 9.3 %copy-start.3 = (bf16[32,2048]{1,0:T(8,128)(2,1)S(1)}, bf16[32,2048]{1,0:T(8,128)(2,1)}, u32[]{:S(2)}) copy-start(bf16[32,2048]{1,0:T(8,128)(2,1)} %get-tuple-element.298) | copy-start | bytes 393220 | tf_op jit(solution)/shard_map/while
  (1 other events, 1.8 us)
Sparse Core Ops, SparseCore 0:
  9.7 49.1 all-gather.2
  61.4 57.5 all-gather.4
  123.0 99.8 reduce-scatter.6
  340.8 49.0 reduce-scatter.4
where the time goes:
time: 400 us; the launch traced here: 398 us
  waiting for transfers between devices  117 us (29%)
  matrix products  112 us (28%)
  local copies, waits for them, and re-layouts  82.8 us (21%)
  other arithmetic  57.2 us (14%)
  between operations  14.1 us (4%)
  starting transfers between devices  12.3 us (3%)
    dot_general x8, matrix products, one_block(): jnp.dot(flat_weight, columns, preferred_element_type=jnp.float32)  69.5 us
    while x56, local copies, waits for them, and re-layouts  51.2 us
    reduce_scatter x1, waiting for transfers between devices, on_device(): lax.psum_scatter(weight_sum, 'row', scatter_dimension=2, tiled=True) * scale  45.4 us
    while x208, other arithmetic  45.3 us
    all_gather x1, waiting for transfers between devices, on_device(): shard_rows = lax.all_gather(input_rim, 'col', axis=0, tiled=True)  42.7 us
    dot_general x8, matrix products, one_block(): lax.dot_general(columns, grad_rows, (((1,), (1,)), ((), ())), preferred_e...  34.4 us
    all_gather x1, waiting for transfers between devices, on_device(): gathered_weight = lax.all_gather(weight, 'row', axis=2, tiled=True)  24.3 us
    unnamed x7, local copies, waits for them, and re-layouts  14.7 us
  transfers between devices with their start and end apart: 8, of which 6 were waited for; matrix products, arithmetic and copies ran while one was open for 50% of the time, Pallas kernels for 0%

commit v1 on v0

v1 whole, which is shorter than its diff:
```python
import math

import jax
import jax.numpy as jnp
from jax import lax
from jax.experimental import pallas as pl
from jax.experimental.pallas import tpu as pltpu
from jax.sharding import PartitionSpec as P

BX = 32
BY = 32
N = BX * BY
MESH = pl.DeviceIdType.MESH
f32 = jnp.float32
bf16 = jnp.bfloat16
SHIFTS = [(b, e) for b in (-1, 0, 1) for e in (-1, 0, 1)]
NX, NY, NZ = 4, 4, 8
SLICES = 4
SL = 2048 // SLICES
NMSG = 128


def valid(dy, dx):
    lane = lax.broadcasted_iota(jnp.int32, (1, N), 1)
    y = lane // BX + dy
    x = lane % BX + dx
    return (y >= 0) & (y < BY) & (x >= 0) & (x < BX)


def kernel(x_in, w_in, g_in, out_ref, gi_ref, gw_ref,
           xf, wf, wt, mg, gip, gwp, yv, halo, r0, ra, rb, rg, edge_s, edge_r, ssem, rsem):
    r = lax.axis_index("row")
    c = lax.axis_index("col")
    x, y, k = c // 8, (c // 2) % 4, c % 2
    p = x * (1 - k) + y * k
    q = y * (1 - k) + x * k
    sa, sb = 8 - 6 * k, 2 + 6 * k

    def col(pp, qq):
        return lax.rem(pp + 8, 4) * sa + lax.rem(qq + 8, 4) * sb + k

    right_a, left_a = (r, col(p + 1, q)), (r, col(p - 1, q))
    right_b, left_b = (r, col(p, q + 1)), (r, col(p, q - 1))
    up, down = (lax.rem(r + 1, NZ), c), (lax.rem(r + 7, NZ), c)
    twin = (r, c + 1 - 2 * k)

    barrier = pltpu.get_barrier_semaphore()
    for peer in (right_a, left_a, right_b, left_b, up, down, twin):
        pl.semaphore_signal(barrier, inc=1, device_id=peer, device_id_type=MESH)
    pl.semaphore_wait(barrier, 7)

    made = []

    def send(src, dst, peer):
        i = len(made)
        copy = pltpu.make_async_remote_copy(
            src_ref=src, dst_ref=dst, send_sem=ssem.at[i], recv_sem=rsem.at[i],
            device_id=peer, device_id_type=MESH)
        copy.start()
        made.append(copy)
        return copy

    def rows(base, size, unit):
        return pl.ds(pl.multiple_of(base, unit), size)

    def block(pp, qq, half=None):
        base = col(pp, qq) * 32
        if half is None:
            return xf.at[rows(base, 32, 32)]
        return xf.at[rows(base + 16 * half, 16, 16)]

    def wcols(rr):
        return rows(lax.rem(rr + 16, NZ) * 128, 128, 128)

    h_up = send(g_in.at[1], halo.at[0], up)
    h_dn = send(g_in.at[0], halo.at[1], down)
    a0 = send(x_in, block(p, q), right_a)
    a1 = send(x_in, block(p, q), left_a)
    b0 = {0: send(x_in, block(p, q), right_b)}
    b1 = {0: send(x_in, block(p, q), left_b)}
    wu = [send(w_in, wf.at[:, wcols(r)], up)]
    wd = [send(w_in, wf.at[:, wcols(r)], down)]
    tw = [send(x_in, block(p, q), twin)]
    xf[rows(c * 32, 32, 32), :] = x_in[...]
    wf[:, wcols(r)] = w_in[...]

    def build(src, plane):
        for j, (b, e) in enumerate(SHIFTS):
            s = (b * BX + e) % N
            v = src
            if s:
                v = jnp.where(valid(-b, -e), pltpu.roll(src, s, 1), 0.0)
            v = v.astype(bf16)
            for a in (-1, 0, 1):
                if plane + a in (0, 1):
                    lo = (a + 1) * 288 + j * 32
                    mg[lo:lo + 32, (plane + a) * N:(plane + a + 1) * N] = v

    def turn(rr):
        rr = lax.rem(rr + 16, NZ)
        blk = wf[:, rows(rr * 128, 128, 128)].T
        for i in range(4):
            core, dy = i % 2, i // 2
            xx, yy = rr // 2, 2 * lax.rem(rr, 2) + dy
            pos = core * 16 + (xx * 4 + yy if core == 0 else yy * 4 + xx)
            wt[rows(pos * 32, 32, 32), 0:864] = blk[i * 32:(i + 1) * 32]

    def forward_a(copy, d, back):
        copy.wait_recv()
        half = send(block(p + d, q, back), block(p + d, q, back), right_a if d < 0 else left_a)
        b0[d] = send(block(p + d, q), block(p + d, q), right_b)
        b1[d] = send(block(p + d, q), block(p + d, q), left_b)
        tw.append(send(block(p + d, q), block(p + d, q), twin))
        return half

    halves = {}

    def forward_b(d):
        b0[d].wait_recv()
        u = send(block(p + d, q - 1, 0), block(p + d, q - 1, 0), right_b)
        tw.append(send(block(p + d, q - 1), block(p + d, q - 1), twin))
        b1[d].wait_recv()
        v = send(block(p + d, q + 1, 1), block(p + d, q + 1, 1), left_b)
        tw.append(send(block(p + d, q + 1), block(p + d, q + 1), twin))
        halves[d] = (u, v)

    def finish_b(d):
        halves[d][0].wait_recv()
        halves[d][1].wait_recv()
        tw.append(send(block(p + d, q + 2), block(p + d, q + 2), twin))

    def forward_w(step):
        wu[-1].wait_recv()
        wd[-1].wait_recv()
        lo, hi = wcols(r - step), wcols(r + step)
        if step < 3:
            wu.append(send(wf.at[:, lo], wf.at[:, lo], up))
            wd.append(send(wf.at[:, hi], wf.at[:, hi], down))
        else:
            wu.append(send(wf.at[0:432, lo], wf.at[0:432, lo], up))
            wd.append(send(wf.at[432:864, hi], wf.at[432:864, hi], down))

    a2 = forward_a(a0, -1, 0)
    a3 = forward_a(a1, 1, 1)
    build(g_in[0].astype(f32), 0)
    forward_b(0)
    a2.wait_recv()
    a3.wait_recv()
    b0[2] = send(block(p + 2, q), block(p + 2, q), right_b)
    b1[2] = send(block(p + 2, q), block(p + 2, q), left_b)
    tw.append(send(block(p + 2, q), block(p + 2, q), twin))
    build(g_in[1].astype(f32), 1)
    forward_b(-1)
    forward_w(1)
    forward_b(1)
    finish_b(0)
    h_up.wait_recv()
    build(jnp.where(r == 0, 0.0, halo[0].astype(f32)), -1)
    finish_b(-1)
    forward_b(2)
    h_dn.wait_recv()
    build(jnp.where(r == NZ - 1, 0.0, halo[1].astype(f32)), 2)
    finish_b(1)
    finish_b(2)
    turn(r)
    turn(r - 1)
    turn(r + 1)
    forward_w(2)
    for copy in tw:
        copy.wait_recv()

    def gw_tile(i, carry):
        lo = rows(i * 256, 256, 256)
        for m in range(2):
            gwp[m * 432:(m + 1) * 432, lo] = lax.dot_general(
                mg[m * 432:(m + 1) * 432, :], xf[lo, :], (((1,), (1,)), ((), ())),
                preferred_element_type=f32)
        return carry

    lax.fori_loop(0, 2, gw_tile, 0)
    forward_w(3)
    lax.fori_loop(2, 4, gw_tile, 0)

    top, bot = (0, 432), (432, 432)

    def gpart(d, half):
        return (pl.ds(*half), wcols(r + d))

    sent_u, sent_d = [], []

    def gw_send(direction, d, half):
        sent = sent_u if direction > 0 else sent_d
        slot = rg.at[0 if direction > 0 else 1, len(sent)]
        sent.append(send(gwp.at[gpart(d, half)], slot, up if direction > 0 else down))

    def gw_step(i):
        for direction, sent in ((1, sent_u), (-1, sent_d)):
            first, second = (top, bot) if direction > 0 else (bot, top)
            half = first if i % 2 == 0 else second
            d = direction * (3 - (i + 1) // 2)
            sent[i].wait_recv()
            at = gpart(d, half)
            gwp[at] = gwp[at] + rg[0 if direction > 0 else 1, i]
            if d != 0:
                gw_send(direction, d, half)

    gw_send(1, 4, top)
    gw_send(-1, -4, bot)
    gw_send(1, 3, bot)
    gw_send(-1, -3, top)

    for d in (-2, 2, -3, 3):
        turn(r + d)
    wu[-1].wait_recv()
    wd[-1].wait_recv()
    turn(r + 4)

    mine, other = k * 512, (1 - k) * 512

    def gi_slice(l):
        for t in range(SL // 256):
            lo = l * SL + t * 256
            for m in range(2):
                gip[m * 512:(m + 1) * 512, lo:lo + 256] = jnp.dot(
                    wt[m * 512:(m + 1) * 512, 0:864], mg[:, lo:lo + 256], preferred_element_type=f32)
        at = pl.ds(l * SL, SL)
        return send(gip.at[rows(other, 512, 512), at], r0.at[:, at], twin)

    def pass_one(l, base, unit, pos, right, left, buf):
        half = unit // 2
        at = pl.ds(l * SL, SL)

        def part(d, which):
            return (rows(base + lax.rem(pos + d + 8, 4) * unit + which * half, half, half), at)

        def go(i, d, which, peer):
            return send(gip.at[part(d, which)], buf.at[i, :, at], peer)

        first = [go(0, 2, 0, right), go(1, 2, 1, left), go(2, 1, 1, right), go(3, -1, 0, left)]

        def second():
            first[0].wait_recv()
            here = part(1, 0)
            gip[here] = gip[here] + buf[0, :, at]
            first.append(go(4, 1, 0, right))
            first[1].wait_recv()
            here = part(-1, 1)
            gip[here] = gip[here] + buf[1, :, at]
            first.append(go(5, -1, 1, left))

        def third():
            first[2].wait_recv()
            first[5].wait_recv()
            here = part(0, 1)
            gip[here] = gip[here] + (buf[2, :, at] + buf[5, :, at])
            first[3].wait_recv()
            first[4].wait_recv()
            here = part(0, 0)
            gip[here] = gip[here] + (buf[3, :, at] + buf[4, :, at])

        return second, third

    pair, stage_a, stage_b = {}, {}, {}

    def join(l):
        pair[l].wait_recv()
        here = (rows(mine, 512, 512), pl.ds(l * SL, SL))
        gip[here] = gip[here] + r0[:, pl.ds(l * SL, SL)]
        stage_a[l] = pass_one(l, mine, 128, p, right_a, left_a, ra)

    def step_b(l):
        stage_a[l][1]()
        stage_b[l] = pass_one(l, mine + p * 128, 32, q, right_b, left_b, rb)

    pair[0] = gi_slice(0)
    pair[1] = gi_slice(1)
    join(0)
    gw_step(0)
    pair[2] = gi_slice(2)
    join(1)
    stage_a[0][0]()
    pair[3] = gi_slice(3)
    join(2)
    gw_step(1)
    stage_a[1][0]()
    join(3)
    step_b(0)

    def y_tile(n, carry):
        lo = rows(n * 256, 256, 256)
        for m in range(2):
            yv[m * 432:(m + 1) * 432, lo] = jnp.dot(
                wf[m * 432:(m + 1) * 432, :], xf[:, lo], preferred_element_type=f32)
        return carry

    lax.fori_loop(0, 4, y_tile, 0)
    gw_step(2)
    stage_a[2][0]()
    step_b(1)
    stage_b[0][0]()
    lax.fori_loop(4, 8, y_tile, 0)
    stage_a[3][0]()
    gw_step(3)

    def plane(z):
        acc = None
        for j, (b, e) in enumerate(SHIFTS):
            t = None
            for a in (-1, 0, 1):
                if z + a in (0, 1):
                    lo = (a + 1) * 288 + j * 32
                    u = yv[lo:lo + 32, (z + a) * N:(z + a + 1) * N]
                    t = u if t is None else t + u
            s = (-(b * BX + e)) % N
            if s:
                t = jnp.where(valid(b, e), pltpu.roll(t, s, 1), 0.0)
            acc = t if acc is None else acc + t
        return acc

    edge_s[0] = plane(-1)
    e_dn = send(edge_s.at[0], edge_r.at[0], down)
    edge_s[1] = plane(2)
    e_up = send(edge_s.at[1], edge_r.at[1], up)
    step_b(2)
    stage_b[1][0]()
    gw_step(4)
    own0 = plane(0)
    own1 = plane(1)
    step_b(3)
    stage_b[0][1]()
    stage_b[2][0]()
    e_up.wait_recv()
    out_ref[0] = (own0 + jnp.where(r == 0, 0.0, edge_r[1])).astype(bf16)
    e_dn.wait_recv()
    out_ref[1] = (own1 + jnp.where(r == NZ - 1, 0.0, edge_r[0])).astype(bf16)
    stage_b[1][1]()
    stage_b[3][0]()
    stage_b[2][1]()
    stage_b[3][1]()
    gi_ref[...] = gip[rows(mine + p * 128 + q * 32, 32, 32), :].astype(bf16)
    gw_step(5)
    gw_step(6)
    gw_ref[...] = gwp[:, wcols(r)] * (1.0 / math.sqrt(16 * N))
    for copy in made:
        copy.wait_send()


def on_device(inputs, weight, grad_out):
    xr = inputs.reshape(32, 2 * N)
    wr = weight.transpose(1, 0, 2).reshape(27 * 32, 128)
    gr = grad_out.transpose(1, 0, 2)
    vm = pl.BlockSpec(memory_space=pltpu.VMEM)
    out, gi, gw = pl.pallas_call(
        kernel,
        out_shape=(jax.ShapeDtypeStruct((2, 32, N), bf16),
                   jax.ShapeDtypeStruct((32, 2 * N), bf16),
                   jax.ShapeDtypeStruct((864, 128), f32)),
        in_specs=[vm] * 3,
        out_specs=(vm,) * 3,
        scratch_shapes=[
            pltpu.VMEM((1024, 2 * N), bf16),
            pltpu.VMEM((864, 1024), bf16),
            pltpu.VMEM((1024, 896), bf16),
            pltpu.VMEM((864, 2 * N), bf16),
            pltpu.VMEM((1024, 2 * N), f32),
            pltpu.VMEM((864, 1024), f32),
            pltpu.VMEM((864, 2 * N), f32),
            pltpu.VMEM((2, 32, N), bf16),
            pltpu.VMEM((512, 2 * N), f32),
            pltpu.VMEM((6, 64, 2 * N), f32),
            pltpu.VMEM((6, 16, 2 * N), f32),
            pltpu.VMEM((2, 7, 432, 128), f32),
            pltpu.VMEM((2, 32, N), f32),
            pltpu.VMEM((2, 32, N), f32),
            pltpu.SemaphoreType.DMA((NMSG,)),
            pltpu.SemaphoreType.DMA((NMSG,)),
        ],
        compiler_params=pltpu.CompilerParams(
            collective_id=0, has_side_effects=True, vmem_limit_bytes=58 << 20),
        name="layer",
    )(xr, wr, gr)
    return (out.transpose(1, 0, 2), gi.reshape(32, 2, N),
            gw.reshape(27, 32, 128).transpose(1, 0, 2))


def solution(mesh):
    placed = (P("col", "row", None), P("col", None, "row"), P("col", "row", None))
    return jax.shard_map(on_device, mesh=mesh, in_specs=placed, out_specs=placed[:1] * 2 + placed[1:2], check_vma=False)
```

time: 400 us -> 84.7 us (0.21)
  waiting for transfers between devices: 117 us -> 0 us
  matrix products: 112 us -> 0 us
  Pallas kernels: 0 us -> 76.9 us
  local copies, waits for them, and re-layouts: 82.8 us -> 6.45 us
  other arithmetic: 57.2 us -> 0 us
  between operations: 14.1 us -> 0.66 us
  starting transfers between devices: 12.3 us -> 0 us
    dot_general x17 -> x0, matrix products: 112 us -> none  [the longest x8 69.5 us: one_block(): jnp.dot(flat_weight, columns, preferred_element_type=jnp.float32)]
    pallas_call x0 -> x1, Pallas kernels: none -> 76.9 us  [on_device(): pl.pallas_call(kernel, out_shape=(jax.ShapeDtypeStruct((2, 32, N), bf16),...]
    all_gather x2 -> x0, waiting for transfers between devices: 67 us -> none  [the longest x1 42.7 us: on_device(): shard_rows = lax.all_gather(input_rim, 'col', axis=0, tiled=True)]
    while x56 -> x0, local copies, waits for them, and re-layouts: 51.2 us -> none
    reduce_scatter x1 -> x0, waiting for transfers between devices: 45.4 us -> none  [on_device(): lax.psum_scatter(weight_sum, 'row', scatter_dimension=2, tiled=True) * scale]
    while x208 -> x0, other arithmetic: 45.3 us -> none
    dynamic_slice x8 -> x0, local copies, waits for them, and re-layouts: 12.8 us -> none  [one_block(): lax.dynamic_slice_in_dim(shard_rows, b * block_rows, block_rows, 0)]
    ppermute x4 -> x0, starting transfers between devices: 12.2 us -> none  [the longest x2 9.58 us: extended(): lax.ppermute(lax.slice_in_dim(block, block.shape[dim] - width, None, axis...]
  transfers between devices with their start and end apart: 8 -> 0, of which waited for: 6 -> 0; matrix products, arithmetic and copies ran while one was open for 50% -> 0% of each run, Pallas kernels for 0% -> 0%
where the time goes in v1:
time: 84.7 us; the launch traced here: 84 us
  Pallas kernels  76.9 us (91%)
  local copies, waits for them, and re-layouts  6.45 us (8%)
    pallas_call x1, Pallas kernels, on_device(): pl.pallas_call(kernel, out_shape=(jax.ShapeDtypeStruct((2, 32, N), bf16),...  76.9 us
    unnamed x8, local copies, waits for them, and re-layouts  4.82 us

profile of v1, /device:TPU:8, one launch (start us, length us, event | category | flops | bytes accessed | tf_op | source)
XLA Modules:
  0.0 84.0 jit_solution(14891122404146742262)
XLA Ops:
  0.6 0.0 copy-start.1
  0.6 1.6 %copy.8 = bf16[4,8,2,1024]{3,1,2,0:T(8,128)(2,1)} copy(bf16[4,8,2,1024]{3,2,1,0:T(2,128)(2,1)} %bitcast.16) | data formatting | bytes 262144
  2.3 0.0 copy-done.1
  2.3 0.7 copy.10
  2.9 76.9 %layer.1 = (bf16[2,32,1024]{2,1,0:T(8,128)(2,1)}, bf16[32,2048]{1,0:T(8,128)(2,1)}, f32[864,128]{1,0:T(8,128)}) custom-call(bf16[32,2048]{1,0:T(8,128)(2,1)} %bitcast.12, bf16[864,128]{1,0:T(8,128)(2,1)} %bitcast.15, bf16[2,32,1024]{2,1,0:T(8,128)(2,1)} %bitcast.13), custom_call_target="tpu_custom_call" | custom-call | tf_op jit(solution)/shard_map/layer/pallas_call | solution.py:353
  79.9 0.0 copy-start
  79.9 1.7 %copy.7 = bf16[32,2,1024]{2,1,0:T(2,128)(2,1)} copy(bf16[32,2,1024]{2,0,1:T(8,128)(2,1)} %bitcast.17) | data formatting | bytes 262144
  81.6 1.6 %reshape.20 = bf16[32,2,1024]{2,1,0:T(2,128)(2,1)} reshape(bf16[32,2048]{1,0:T(8,128)(2,1)} %get-tuple-element.7) | data formatting | bytes 262144 | tf_op jit(solution)/shard_map/reshape | solution.py:382
  83.3 0.0 copy-done
  83.3 0.8 copy.12
Async XLA Ops:
  0.6 1.6 %copy-start.1 = (bf16[32,2,1024]{2,1,0:T(2,128)(2,1)S(1)}, bf16[32,2,1024]{2,1,0:T(2,128)(2,1)}, u32[]{:S(2)}) copy-start(bf16[32,2,1024]{2,1,0:T(2,128)(2,1)} %param.5) | copy-start | bytes 393220
  79.9 3.4 %copy-start = (f32[864,128]{1,0:T(8,128)S(1)}, f32[864,128]{1,0:T(8,128)}, u32[]{:S(2)}) copy-start(f32[864,128]{1,0:T(8,128)} %get-tuple-element.8) | copy-start | bytes 1327108

commit v2 on v1

v2 whole, which is shorter than its diff:
```python
import math

import jax
import jax.numpy as jnp
from jax import lax
from jax.experimental import pallas as pl
from jax.experimental.pallas import tpu as pltpu
from jax.sharding import PartitionSpec as P

BX = 32
BY = 32
N = BX * BY
MESH = pl.DeviceIdType.MESH
f32 = jnp.float32
bf16 = jnp.bfloat16
SHIFTS = [(b, e) for b in (-1, 0, 1) for e in (-1, 0, 1)]
NX, NY, NZ = 4, 4, 8
SLICES = 4
SL = 2048 // SLICES
NMSG = 208
SCHED = (
    "s0", "t1", "s1", "s2", "j0", "g0", "t2", "y0", "s3", "j1", "a0", "g1", "y1", "y2",
    "t3", "j2", "a1", "b0", "g2", "y3", "y4", "y5", "j3", "a2", "b1", "c0", "g3", "y6",
    "y7", "p-1", "a3", "b2", "c1", "f0", "g4", "p2", "b3", "c2", "f1", "p0", "c3", "f2",
    "g5", "p1", "f3", "o0", "o1", "g6",
)


def valid(dy, dx):
    lane = lax.broadcasted_iota(jnp.int32, (1, N), 1)
    y = lane // BX + dy
    x = lane % BX + dx
    return (y >= 0) & (y < BY) & (x >= 0) & (x < BX)


def kernel(x_in, w_in, g_in, out_ref, gi_ref, gw_ref,
           xf, wf, wt, mg, gip, gwp, yv, halo, r0, ra, rb, rg, sg, edge_s, edge_r, ssem, rsem):
    r = lax.axis_index("row")
    c = lax.axis_index("col")
    x, y, k = c // 8, (c // 2) % 4, c % 2
    p = x * (1 - k) + y * k
    q = y * (1 - k) + x * k
    sa, sb = 8 - 6 * k, 2 + 6 * k

    def col(pp, qq):
        return lax.rem(pp + 8, 4) * sa + lax.rem(qq + 8, 4) * sb + k

    right_a, left_a = (r, col(p + 1, q)), (r, col(p - 1, q))
    right_b, left_b = (r, col(p, q + 1)), (r, col(p, q - 1))
    up, down = (lax.rem(r + 1, NZ), c), (lax.rem(r + 7, NZ), c)
    twin = (r, c + 1 - 2 * k)

    barrier = pltpu.get_barrier_semaphore()
    for peer in (right_a, left_a, right_b, left_b, up, down, twin):
        pl.semaphore_signal(barrier, inc=1, device_id=peer, device_id_type=MESH)
    pl.semaphore_wait(barrier, 7)

    made = []

    def send(src, dst, peer):
        i = len(made)
        copy = pltpu.make_async_remote_copy(
            src_ref=src, dst_ref=dst, send_sem=ssem.at[i], recv_sem=rsem.at[i],
            device_id=peer, device_id_type=MESH)
        copy.start()
        made.append(copy)
        return copy

    def rows(base, size, unit):
        return pl.ds(pl.multiple_of(base, unit), size)

    def block(pp, qq):
        return xf.at[rows(col(pp, qq) * 32, 32, 32)]

    def unit(pp, qq, h):
        return xf.at[rows(col(pp, qq) * 32 + 16 * h, 16, 16)]

    def wcols(rr):
        return rows(lax.rem(rr + 16, NZ) * 128, 128, 128)

    ar, al, fa = {}, {}, {}
    br, bl, fb = {}, {}, {}
    tw = []
    h_up = send(g_in.at[1], halo.at[0], up)
    h_dn = send(g_in.at[0], halo.at[1], down)
    for h in (0, 1):
        src = x_in.at[16 * h:16 * h + 16]
        other_src = x_in.at[16 - 16 * h:32 - 16 * h]
        ar[h] = send(src, unit(p, q, h), right_a)
        al[1 - h] = send(other_src, unit(p, q, 1 - h), left_a)
        br[0, h] = send(src, unit(p, q, h), right_b)
        bl[0, 1 - h] = send(other_src, unit(p, q, 1 - h), left_b)
    wu, wd = {}, {}
    for i in (0, 1):
        for step, got, peer in ((i, wu, up), (1 - i, wd, down)):
            got[0, step] = send(w_in.at[432 * step:432 * step + 432],
                                wf.at[432 * step:432 * step + 432, wcols(r)], peer)
    tw.append(send(x_in, block(p, q), twin))
    xf[rows(c * 32, 32, 32), :] = x_in[...]
    wf[:, wcols(r)] = w_in[...]

    def build(src, plane):
        for j, (b, e) in enumerate(SHIFTS):
            s = (b * BX + e) % N
            v = src
            if s:
                v = jnp.where(valid(-b, -e), pltpu.roll(src, s, 1), 0.0)
            v = v.astype(bf16)
            for a in (-1, 0, 1):
                if plane + a in (0, 1):
                    lo = (a + 1) * 288 + j * 32
                    mg[lo:lo + 32, (plane + a) * N:(plane + a + 1) * N] = v

    def gi_turn(j):
        blk = wf[:, rows(lax.rem(j + 8, 4) * 256, 256, 256)].T
        for i in range(8):
            to = (i % 2) * 128 + (i // 2) * 32
            wt[to:to + 32, 0:864] = blk[i * 32:(i + 1) * 32]

    def gi_pair(j, start, tiles):
        jj = lax.rem(j + 8, 4)

        def tile(n, carry):
            o = jnp.dot(wt[:, 0:864], mg[:, rows(n * SL, SL, SL)], preferred_element_type=f32)
            gip[n, rows(jj * 128, 128, 128), :] = o[0:128]
            for i in range(4):
                gip[n, rows(512 + i * 128 + jj * 32, 32, 32), :] = o[128 + i * 32:160 + i * 32]
            return carry

        lax.fori_loop(start, start + tiles, tile, 0)

    half_r = r // 2
    sign = 1 - 2 * lax.rem(r, 2)

    def spread_b(d, h):
        u = unit(p + d, q, h)
        if h == 0:
            br[d, h] = send(u, u, right_b)
            bl[d, h] = send(u, u, left_b)
        else:
            bl[d, h] = send(u, u, left_b)
            br[d, h] = send(u, u, right_b)

    def share(pp, qq):
        tw.append(send(block(pp, qq), block(pp, qq), twin))

    def take_a(d, h):
        (ar if d < 0 else al)[h].wait_recv()
        u = unit(p + d, q, h)
        if (d, h) == (-1, 0):
            fa[0] = send(u, u, right_a)
        if (d, h) == (1, 1):
            fa[1] = send(u, u, left_a)
        spread_b(d, h)

    def take_b(d):
        br[d, 0].wait_recv()
        u = unit(p + d, q - 1, 0)
        fb[d, 0] = send(u, u, right_b)
        bl[d, 1].wait_recv()
        u = unit(p + d, q + 1, 1)
        fb[d, 1] = send(u, u, left_b)

    def rest_b(d):
        br[d, 1].wait_recv()
        share(p + d, q - 1)
        bl[d, 0].wait_recv()
        share(p + d, q + 1)

    def finish_b(d):
        fb[d, 0].wait_recv()
        fb[d, 1].wait_recv()
        share(p + d, q + 2)

    def forward_w(step, i):
        for got, peer, part, d in ((wu, up, i, -step), (wd, down, 1 - i, step)):
            got[step - 1, part].wait_recv()
            if step < 3 or (step == 3 and i == 0):
                here = wf.at[432 * part:432 * part + 432, wcols(r + d)]
                got[step, part] = send(here, here, peer)

    build(g_in[0].astype(f32), 0)
    take_a(-1, 0)
    take_a(1, 1)
    take_b(0)
    forward_w(1, 0)
    take_a(-1, 1)
    share(p - 1, q)
    take_a(1, 0)
    share(p + 1, q)
    for h in (0, 1):
        fa[h].wait_recv()
        spread_b(2, h)
    share(p + 2, q)
    rest_b(0)
    build(g_in[1].astype(f32), 1)
    take_b(-1)
    take_b(1)
    forward_w(1, 1)
    h_up.wait_recv()
    build(jnp.where(r == 0, 0.0, halo[0].astype(f32)), -1)
    finish_b(0)
    rest_b(-1)
    rest_b(1)
    forward_w(2, 0)
    h_dn.wait_recv()
    build(jnp.where(r == NZ - 1, 0.0, halo[1].astype(f32)), 2)
    take_b(2)
    gi_turn(half_r)
    forward_w(2, 1)
    finish_b(-1)
    finish_b(1)
    rest_b(2)
    gi_pair(half_r, 0, 2)
    forward_w(3, 0)
    gi_pair(half_r, 2, 2)
    finish_b(2)
    gi_turn(half_r - sign)
    gi_pair(half_r - sign, 0, 2)
    forward_w(3, 1)
    gi_pair(half_r - sign, 2, 2)
    gi_turn(half_r + sign)
    for copy in tw:
        copy.wait_recv()

    def gw_tile(j):
        lo = rows(lax.rem(j + 8, 4) * 256, 256, 256)

        def part(m, carry):
            at = rows(m * 432, 432, 16)
            gwp[at, lo] = lax.dot_general(
                mg[at, :], xf[lo, :], (((1,), (1,)), ((), ())), preferred_element_type=f32)
            return carry

        lax.fori_loop(0, 2, part, 0)

    top, bot = (0, 448), (448, 416)

    def gpart(d, half):
        return (pl.ds(*half), wcols(r + d))

    def pack(v, dst):
        n = v.shape[0]
        hi = v.astype(bf16)
        h = hi.astype(f32)
        big = jnp.abs(h) > 1e-34
        t = jnp.where(big, (v - h) / jnp.where(big, h, 1.0), 0.0)
        lev = jnp.floor(t * 2560.0 + 0.5)
        dst[0:n] = hi
        dst[n:n + n // 2] = (lev[:n // 2] * 21.0 + lev[n // 2:]).astype(bf16)

    def unpack(src, n):
        h = src[0:n].astype(f32)
        both = src[n:n + n // 2].astype(f32)
        first = jnp.floor((both + 10.5) * (1.0 / 21.0))
        lev = jnp.concatenate([first, both - 21.0 * first], axis=0)
        return h + h * (lev * (1.0 / 2560.0))

    sent_u, sent_d = [], []

    def gw_send(direction, d, half, v=None):
        sent = sent_u if direction > 0 else sent_d
        side, i, n = (1 - direction) // 2, len(sent), half[1]
        pack(gwp[gpart(d, half)] if v is None else v, sg.at[side, i])
        sent.append(send(sg.at[side, i, 0:n + n // 2], rg.at[side, i, 0:n + n // 2],
                         up if direction > 0 else down))

    def gw_step(i):
        for direction, sent in ((1, sent_u), (-1, sent_d)):
            first, second = (top, bot) if direction > 0 else (bot, top)
            half = first if i % 2 == 0 else second
            d = direction * (3 - (i + 1) // 2)
            sent[i].wait_recv()
            at = gpart(d, half)
            v = gwp[at] + unpack(rg.at[(1 - direction) // 2, i], half[1])
            if d != 0:
                gw_send(direction, d, half, v)
            else:
                gwp[at] = v

    gw_tile(half_r + 2)
    gw_send(1, 4, top)
    gw_send(-1, -4, bot)
    gi_pair(half_r + sign, 0, 4)
    forward_w(4, 0)
    gi_turn(half_r + 2)

    mine, other = k * 512, (1 - k) * 512

    def gi_slice(l):
        gi_pair(half_r + 2, l, 1)
        return send(gip.at[l, rows(other, 512, 512)], r0.at[l], twin)

    def pass_one(l, base, unit, pos, right, left, buf):
        half = unit // 2

        def part(d, which):
            return (l, rows(base + lax.rem(pos + d + 8, 4) * unit + which * half, half, half))

        def go(i, d, which, peer):
            return send(gip.at[part(d, which)], buf.at[l, i], peer)

        first = [go(0, 2, 0, right), go(1, 2, 1, left), go(2, 1, 1, right), go(3, -1, 0, left)]

        def second():
            first[0].wait_recv()
            here = part(1, 0)
            gip[here] = gip[here] + buf[l, 0]
            first.append(go(4, 1, 0, right))
            first[1].wait_recv()
            here = part(-1, 1)
            gip[here] = gip[here] + buf[l, 1]
            first.append(go(5, -1, 1, left))

        def third():
            first[2].wait_recv()
            first[5].wait_recv()
            here = part(0, 1)
            gip[here] = gip[here] + (buf[l, 2] + buf[l, 5])
            first[3].wait_recv()
            first[4].wait_recv()
            here = part(0, 0)
            gip[here] = gip[here] + (buf[l, 3] + buf[l, 4])

        return second, third

    pair, stage_a, stage_b = {}, {}, {}

    def join(l):
        pair[l].wait_recv()
        here = (l, rows(mine, 512, 512))
        gip[here] = gip[here] + r0[l]
        stage_a[l] = pass_one(l, mine, 128, p, right_a, left_a, ra)

    def step_b(l):
        stage_a[l][1]()
        stage_b[l] = pass_one(l, mine + p * 128, 32, q, right_b, left_b, rb)

    def y_tile(n, carry):
        lo = rows(n * 256, 256, 256)
        for m in range(2):
            yv[m * 432:(m + 1) * 432, lo] = jnp.dot(
                wf[m * 432:(m + 1) * 432, :], xf[:, lo], preferred_element_type=f32)
        return carry


    def ys(lo, hi):
        lax.fori_loop(lo, hi, y_tile, 0)

    def plane(z):
        acc = None
        for j, (b, e) in enumerate(SHIFTS):
            t = None
            for a in (-1, 0, 1):
                if z + a in (0, 1):
                    lo = (a + 1) * 288 + j * 32
                    u = yv[lo:lo + 32, (z + a) * N:(z + a + 1) * N]
                    t = u if t is None else t + u
            s = (-(b * BX + e)) % N
            if s:
                t = jnp.where(valid(b, e), pltpu.roll(t, s, 1), 0.0)
            acc = t if acc is None else acc + t
        return acc

    def step_a2(l):
        stage_a[l][0]()

    def step_b2(l):
        stage_b[l][0]()

    def finish(l):
        stage_b[l][1]()

    own, edges = {}, {}

    def step_s(l):
        pair[l] = gi_slice(l)

    def step_t(i):
        gw_tile(half_r + 2 + (0, -sign, sign, 2)[i])
        if i == 1:
            gw_send(1, 3, bot)
            gw_send(-1, -3, top)

    def step_y(n):
        ys(n, n + 1)

    def step_p(z):
        if z in (0, 1):
            own[z] = plane(z)
        else:
            i = (z + 1) // 3
            edge_s[i] = plane(z)
            edges[i] = send(edge_s.at[i], edge_r.at[i], up if i else down)

    def step_o(z):
        edges[1 - z].wait_recv()
        gone = r == (NZ - 1 if z else 0)
        out_ref[z] = (own[z] + jnp.where(gone, 0.0, edge_r[1 - z])).astype(bf16)

    ops = dict(s=step_s, t=step_t, y=step_y, p=step_p, o=step_o, g=gw_step, j=join,
               a=step_a2, b=step_b, c=step_b2, f=finish)
    for word in SCHED:
        ops[word[0]](int(word[1:]))
    for l in range(SLICES):
        gi_ref[:, l * SL:(l + 1) * SL] = gip[l, rows(mine + p * 128 + q * 32, 32, 32), :].astype(bf16)
    gw_ref[...] = gwp[:, wcols(r)] * (1.0 / math.sqrt(16 * N))
    for copy in made:
        copy.wait_send()


def on_device(inputs, weight, grad_out):
    xr = inputs.reshape(32, 2 * N)
    wr = weight.transpose(1, 0, 2).reshape(27 * 32, 128)
    gr = grad_out.transpose(1, 0, 2)
    vm = pl.BlockSpec(memory_space=pltpu.VMEM)
    out, gi, gw = pl.pallas_call(
        kernel,
        out_shape=(jax.ShapeDtypeStruct((2, 32, N), bf16),
                   jax.ShapeDtypeStruct((32, 2 * N), bf16),
                   jax.ShapeDtypeStruct((864, 128), f32)),
        in_specs=[vm] * 3,
        out_specs=(vm,) * 3,
        scratch_shapes=[
            pltpu.VMEM((1024, 2 * N), bf16),
            pltpu.VMEM((864, 1024), bf16),
            pltpu.VMEM((256, 896), bf16),
            pltpu.VMEM((864, 2 * N), bf16),
            pltpu.VMEM((SLICES, 1024, SL), f32),
            pltpu.VMEM((864, 1024), f32),
            pltpu.VMEM((864, 2 * N), f32),
            pltpu.VMEM((2, 32, N), bf16),
            pltpu.VMEM((SLICES, 512, SL), f32),
            pltpu.VMEM((SLICES, 6, 64, SL), f32),
            pltpu.VMEM((SLICES, 6, 16, SL), f32),
            pltpu.VMEM((2, 7, 672, 128), bf16),
            pltpu.VMEM((2, 7, 672, 128), bf16),
            pltpu.VMEM((2, 32, N), f32),
            pltpu.VMEM((2, 32, N), f32),
            pltpu.SemaphoreType.DMA((NMSG,)),
            pltpu.SemaphoreType.DMA((NMSG,)),
        ],
        compiler_params=pltpu.CompilerParams(
            collective_id=0, has_side_effects=True, vmem_limit_bytes=58 << 20),
        name="layer",
    )(xr, wr, gr)
    return (out.transpose(1, 0, 2), gi.reshape(32, 2, N),
            gw.reshape(27, 32, 128).transpose(1, 0, 2))


def solution(mesh):
    placed = (P("col", "row", None), P("col", None, "row"), P("col", "row", None))
    return jax.shard_map(on_device, mesh=mesh, in_specs=placed, out_specs=placed[:1] * 2 + placed[1:2], check_vma=False)
```

time: 84.7 us -> 80.1 us (0.946)
  Pallas kernels: 76.9 us -> 72.8 us
    pallas_call x1, Pallas kernels: 76.9 us -> 72.8 us  [on_device(): pl.pallas_call(kernel, out_shape=(jax.ShapeDtypeStruct((2, 32, N), bf16),...]
where the time goes in v2:
time: 80.1 us; the launch traced here: 79.9 us
  Pallas kernels  72.8 us (91%)
  local copies, waits for them, and re-layouts  6.45 us (8%)
    pallas_call x1, Pallas kernels, on_device(): pl.pallas_call(kernel, out_shape=(jax.ShapeDtypeStruct((2, 32, N), bf16),...  72.8 us
    unnamed x8, local copies, waits for them, and re-layouts  4.82 us
    reshape x1, local copies, waits for them, and re-layouts, on_device(): gi.reshape(32, 2, N)  1.64 us

profile of v2, /device:TPU:8, one launch (start us, length us, event | category | flops | bytes accessed | tf_op | source)
XLA Modules:
  0.0 79.9 jit_solution(12518183411125169023)
XLA Ops:
  0.6 0.0 copy-start.1
  0.6 1.6 %copy.8 = bf16[4,8,2,1024]{3,1,2,0:T(8,128)(2,1)} copy(bf16[4,8,2,1024]{3,2,1,0:T(2,128)(2,1)} %bitcast.16) | data formatting | bytes 262144
  2.3 0.0 copy-done.1
  2.3 0.7 copy.10
  2.9 72.8 %layer.1 = (bf16[2,32,1024]{2,1,0:T(8,128)(2,1)}, bf16[32,2048]{1,0:T(8,128)(2,1)}, f32[864,128]{1,0:T(8,128)}) custom-call(bf16[32,2048]{1,0:T(8,128)(2,1)} %bitcast.12, bf16[864,128]{1,0:T(8,128)(2,1)} %bitcast.15, bf16[2,32,1024]{2,1,0:T(8,128)(2,1)} %bitcast.13), custom_call_target="tpu_custom_call" | custom-call | tf_op jit(solution)/shard_map/layer/pallas_call | solution.py:417
  75.8 0.0 copy-start
  75.8 1.7 %copy.7 = bf16[32,2,1024]{2,1,0:T(2,128)(2,1)} copy(bf16[32,2,1024]{2,0,1:T(8,128)(2,1)} %bitcast.17) | data formatting | bytes 262144
  77.5 1.6 %reshape.20 = bf16[32,2,1024]{2,1,0:T(2,128)(2,1)} reshape(bf16[32,2048]{1,0:T(8,128)(2,1)} %get-tuple-element.7) | data formatting | bytes 262144 | tf_op jit(solution)/shard_map/reshape | solution.py:447
  79.2 0.0 copy-done
  79.2 0.8 copy.12
Async XLA Ops:
  0.6 1.6 %copy-start.1 = (bf16[32,2,1024]{2,1,0:T(2,128)(2,1)S(1)}, bf16[32,2,1024]{2,1,0:T(2,128)(2,1)}, u32[]{:S(2)}) copy-start(bf16[32,2,1024]{2,1,0:T(2,128)(2,1)} %param.5) | copy-start | bytes 393220
  75.8 3.4 %copy-start = (f32[864,128]{1,0:T(8,128)S(1)}, f32[864,128]{1,0:T(8,128)}, u32[]{:S(2)}) copy-start(f32[864,128]{1,0:T(8,128)} %get-tuple-element.8) | copy-start | bytes 1327108

commit v3 on v2

--- a/solution.py
+++ b/solution.py
@@ -19,10 +19,10 @@
 SL = 2048 // SLICES
 NMSG = 208
 SCHED = (
-    "s0", "t1", "s1", "s2", "j0", "g0", "t2", "y0", "s3", "j1", "a0", "g1", "y1", "y2",
-    "t3", "j2", "a1", "b0", "g2", "y3", "y4", "y5", "j3", "a2", "b1", "c0", "g3", "y6",
-    "y7", "p-1", "a3", "b2", "c1", "f0", "g4", "p2", "b3", "c2", "f1", "p0", "c3", "f2",
-    "g5", "p1", "f3", "o0", "o1", "g6",
+    "s0", "s1", "s2", "g0", "j0", "t2", "s3", "j1", "g1", "a0", "y0", "t3", "j2", "a1",
+    "b0", "g2", "y1", "y2", "j3", "a2", "b1", "c0", "g3", "y3", "p-1", "a3", "b2", "c1",
+    "f0", "g4", "p2", "b3", "c2", "f1", "p0", "c3", "f2", "g5", "p1", "f3", "o0", "o1",
+    "g6",
 )
 
 
@@ -83,20 +83,20 @@
     tw = []
     h_up = send(g_in.at[1], halo.at[0], up)
     h_dn = send(g_in.at[0], halo.at[1], down)
+    for z in (0, 1):
+        xf[rows(c * 32, 32, 32), z * N:(z + 1) * N] = x_in[z]
     for h in (0, 1):
-        src = x_in.at[16 * h:16 * h + 16]
-        other_src = x_in.at[16 - 16 * h:32 - 16 * h]
-        ar[h] = send(src, unit(p, q, h), right_a)
-        al[1 - h] = send(other_src, unit(p, q, 1 - h), left_a)
-        br[0, h] = send(src, unit(p, q, h), right_b)
-        bl[0, 1 - h] = send(other_src, unit(p, q, 1 - h), left_b)
+        src, other_src = unit(p, q, h), unit(p, q, 1 - h)
+        ar[h] = send(src, src, right_a)
+        al[1 - h] = send(other_src, other_src, left_a)
+        br[0, h] = send(src, src, right_b)
+        bl[0, 1 - h] = send(other_src, other_src, left_b)
     wu, wd = {}, {}
     for i in (0, 1):
         for step, got, peer in ((i, wu, up), (1 - i, wd, down)):
             got[0, step] = send(w_in.at[432 * step:432 * step + 432],
                                 wf.at[432 * step:432 * step + 432, wcols(r)], peer)
-    tw.append(send(x_in, block(p, q), twin))
-    xf[rows(c * 32, 32, 32), :] = x_in[...]
+    tw.append(send(block(p, q), block(p, q), twin))
     wf[:, wcols(r)] = w_in[...]
 
     def build(src, plane):
@@ -213,13 +213,8 @@
     rest_b(2)
     gi_pair(half_r, 0, 2)
     forward_w(3, 0)
+    finish_b(2)
     gi_pair(half_r, 2, 2)
-    finish_b(2)
-    gi_turn(half_r - sign)
-    gi_pair(half_r - sign, 0, 2)
-    forward_w(3, 1)
-    gi_pair(half_r - sign, 2, 2)
-    gi_turn(half_r + sign)
     for copy in tw:
         copy.wait_recv()
 
@@ -244,7 +239,7 @@
         hi = v.astype(bf16)
         h = hi.astype(f32)
         big = jnp.abs(h) > 1e-34
-        t = jnp.where(big, (v - h) / jnp.where(big, h, 1.0), 0.0)
+        t = (v - h) / jnp.where(big, h, 1.0)
         lev = jnp.floor(t * 2560.0 + 0.5)
         dst[0:n] = hi
         dst[n:n + n // 2] = (lev[:n // 2] * 21.0 + lev[n // 2:]).astype(bf16)
@@ -281,6 +276,13 @@
     gw_tile(half_r + 2)
     gw_send(1, 4, top)
     gw_send(-1, -4, bot)
+    forward_w(3, 1)
+    gw_tile(half_r + 2 - sign)
+    gw_send(1, 3, bot)
+    gw_send(-1, -3, top)
+    gi_turn(half_r - sign)
+    gi_pair(half_r - sign, 0, 4)
+    gi_turn(half_r + sign)
     gi_pair(half_r + sign, 0, 4)
     forward_w(4, 0)
     gi_turn(half_r + 2)
@@ -337,7 +339,7 @@
         stage_b[l] = pass_one(l, mine + p * 128, 32, q, right_b, left_b, rb)
 
     def y_tile(n, carry):
-        lo = rows(n * 256, 256, 256)
+        lo = rows(n * 512, 512, 512)
         for m in range(2):
             yv[m * 432:(m + 1) * 432, lo] = jnp.dot(
                 wf[m * 432:(m + 1) * 432, :], xf[:, lo], preferred_element_type=f32)
@@ -378,9 +380,6 @@
 
     def step_t(i):
         gw_tile(half_r + 2 + (0, -sign, sign, 2)[i])
-        if i == 1:
-            gw_send(1, 3, bot)
-            gw_send(-1, -3, top)
 
     def step_y(n):
         ys(n, n + 1)
@@ -410,7 +409,7 @@
 
 
 def on_device(inputs, weight, grad_out):
-    xr = inputs.reshape(32, 2 * N)
+    xr = inputs.transpose(1, 0, 2)
     wr = weight.transpose(1, 0, 2).reshape(27 * 32, 128)
     gr = grad_out.transpose(1, 0, 2)
     vm = pl.BlockSpec(memory_space=pltpu.VMEM)

time: 80.1 us -> 79.4 us (level); the launches traced: 79.9 us -> 78.2 us
  Pallas kernels: 72.8 us -> 71.7 us
    unnamed x8 -> x4, local copies, waits for them, and re-layouts: 4.82 us -> 2.51 us
    transpose x0 -> x1, local copies, waits for them, and re-layouts: none -> 1.72 us  [on_device(): gr = grad_out.transpose(1, 0, 2)]
    pallas_call x1, Pallas kernels: 72.8 us -> 71.7 us  [on_device(): pl.pallas_call(kernel, out_shape=(jax.ShapeDtypeStruct((2, 32, N), bf16),...]
where the time goes in v3:
time: 79.4 us; the launch traced here: 78.2 us
  Pallas kernels  71.7 us (90%)
  local copies, waits for them, and re-layouts  5.87 us (7%)
    pallas_call x1, Pallas kernels, on_device(): pl.pallas_call(kernel, out_shape=(jax.ShapeDtypeStruct((2, 32, N), bf16),...  71.7 us
    unnamed x4, local copies, waits for them, and re-layouts  2.51 us
    transpose x1, local copies, waits for them, and re-layouts, on_device(): gr = grad_out.transpose(1, 0, 2)  1.72 us
    reshape x1, local copies, waits for them, and re-layouts, on_device(): gi.reshape(32, 2, N)  1.64 us

profile of v3, /device:TPU:8, one launch (start us, length us, event | category | flops | bytes accessed | tf_op | source)
XLA Modules:
  0.0 78.2 jit_solution(15542113442246464159)
XLA Ops:
  0.6 1.7 %copy_bitcast_fusion = (bf16[2,32,1024]{2,1,0:T(8,128)(2,1)}, bf16[2,32,1024]{2,1,0:T(8,128)(2,1)}) fusion(bf16[32,2,1024]{2,1,0:T(2,128)(2,1)} %param.5, bf16[32,2,1024]{2,1,0:T(2,128)(2,1)} %param.3), kind=kLoop, calls=%fused_computation | loop fusion | bytes 524288 | tf_op jit(solution)/shard_map/transpose | solution.py:414
  2.4 71.7 %layer.1 = (bf16[2,32,1024]{2,1,0:T(8,128)(2,1)}, bf16[32,2048]{1,0:T(8,128)(2,1)}, f32[864,128]{1,0:T(8,128)}) custom-call(bf16[2,32,1024]{2,1,0:T(8,128)(2,1)} %get-tuple-element.13.x_in, bf16[864,128]{1,0:T(8,128)(2,1)} %bitcast.12, bf16[2,32,1024]{2,1,0:T(8,128)(2,1)} %get-tuple-element.12.g_in), custom_call_target="tpu_custom_call" | custom-call | tf_op jit(solution)/shard_map/layer/pallas_call | solution.py:416
  74.0 0.0 copy-start
  74.1 1.7 %copy.8 = bf16[32,2,1024]{2,1,0:T(2,128)(2,1)} copy(bf16[32,2,1024]{2,0,1:T(8,128)(2,1)} %bitcast.13) | data formatting | bytes 262144
  75.8 1.6 %reshape.16 = bf16[32,2,1024]{2,1,0:T(2,128)(2,1)} reshape(bf16[32,2048]{1,0:T(8,128)(2,1)} %get-tuple-element.7) | data formatting | bytes 262144 | tf_op jit(solution)/shard_map/reshape | solution.py:446
  77.4 0.0 copy-done
  77.4 0.8 copy.12
Async XLA Ops:
  74.0 3.4 %copy-start = (f32[864,128]{1,0:T(8,128)S(1)}, f32[864,128]{1,0:T(8,128)}, u32[]{:S(2)}) copy-start(f32[864,128]{1,0:T(8,128)} %get-tuple-element.8) | copy-start | bytes 1327108

commit v4 on v3

--- a/solution.py
+++ b/solution.py
@@ -402,7 +402,7 @@
     for word in SCHED:
         ops[word[0]](int(word[1:]))
     for l in range(SLICES):
-        gi_ref[:, l * SL:(l + 1) * SL] = gip[l, rows(mine + p * 128 + q * 32, 32, 32), :].astype(bf16)
+        gi_ref[l * SL // N, :, l * SL % N:l * SL % N + SL] = gip[l, rows(mine + p * 128 + q * 32, 32, 32), :].astype(bf16)
     gw_ref[...] = gwp[:, wcols(r)] * (1.0 / math.sqrt(16 * N))
     for copy in made:
         copy.wait_send()
@@ -416,7 +416,7 @@
     out, gi, gw = pl.pallas_call(
         kernel,
         out_shape=(jax.ShapeDtypeStruct((2, 32, N), bf16),
-                   jax.ShapeDtypeStruct((32, 2 * N), bf16),
+                   jax.ShapeDtypeStruct((2, 32, N), bf16),
                    jax.ShapeDtypeStruct((864, 128), f32)),
         in_specs=[vm] * 3,
         out_specs=(vm,) * 3,
@@ -443,7 +443,7 @@
             collective_id=0, has_side_effects=True, vmem_limit_bytes=58 << 20),
         name="layer",
     )(xr, wr, gr)
-    return (out.transpose(1, 0, 2), gi.reshape(32, 2, N),
+    return (out.transpose(1, 0, 2), gi.transpose(1, 0, 2),
             gw.reshape(27, 32, 128).transpose(1, 0, 2))
 
 

time: 79.4 us -> 79.4 us (level)
    unnamed x4 -> x5, local copies, waits for them, and re-layouts: 2.51 us -> 4.21 us
    reshape x1 -> x0, local copies, waits for them, and re-layouts: 1.64 us -> none  [on_device(): gi.reshape(32, 2, N)]
where the time goes in v4:
time: 79.4 us; the launch traced here: 78.3 us
  Pallas kernels  71.7 us (90%)
  local copies, waits for them, and re-layouts  5.93 us (7%)
    pallas_call x1, Pallas kernels, on_device(): pl.pallas_call(kernel, out_shape=(jax.ShapeDtypeStruct((2, 32, N), bf16),...  71.7 us
    unnamed x5, local copies, waits for them, and re-layouts  4.21 us
    transpose x1, local copies, waits for them, and re-layouts, on_device(): gr = grad_out.transpose(1, 0, 2)  1.72 us

profile of v4, /device:TPU:8, one launch (start us, length us, event | category | flops | bytes accessed | tf_op | source)
XLA Modules:
  0.0 78.3 jit_solution(15841220936324210567)
XLA Ops:
  0.6 1.7 %copy_bitcast_fusion = (bf16[2,32,1024]{2,1,0:T(8,128)(2,1)}, bf16[2,32,1024]{2,1,0:T(8,128)(2,1)}) fusion(bf16[32,2,1024]{2,1,0:T(2,128)(2,1)} %param.5, bf16[32,2,1024]{2,1,0:T(2,128)(2,1)} %param.3), kind=kLoop, calls=%fused_computation | loop fusion | bytes 524288 | tf_op jit(solution)/shard_map/transpose | solution.py:414
  2.4 71.7 %layer.1 = (bf16[2,32,1024]{2,1,0:T(8,128)(2,1)}, bf16[2,32,1024]{2,1,0:T(8,128)(2,1)}, f32[864,128]{1,0:T(8,128)}) custom-call(bf16[2,32,1024]{2,1,0:T(8,128)(2,1)} %get-tuple-element.13.x_in, bf16[864,128]{1,0:T(8,128)(2,1)} %bitcast.13, bf16[2,32,1024]{2,1,0:T(8,128)(2,1)} %get-tuple-element.12.g_in), custom_call_target="tpu_custom_call" | custom-call | tf_op jit(solution)/shard_map/layer/pallas_call | solution.py:416
  74.0 0.0 copy-start
  74.1 1.7 %copy.8 = bf16[32,2,1024]{2,1,0:T(2,128)(2,1)} copy(bf16[32,2,1024]{2,0,1:T(8,128)(2,1)} %bitcast.15) | data formatting | bytes 262144
  75.8 1.7 %copy.9 = bf16[32,2,1024]{2,1,0:T(2,128)(2,1)} copy(bf16[32,2,1024]{2,0,1:T(8,128)(2,1)} %bitcast.14) | data formatting | bytes 262144
  77.5 0.0 copy-done
  77.5 0.8 copy.13
Async XLA Ops:
  74.0 3.5 %copy-start = (f32[864,128]{1,0:T(8,128)S(1)}, f32[864,128]{1,0:T(8,128)}, u32[]{:S(2)}) copy-start(f32[864,128]{1,0:T(8,128)} %get-tuple-element.8) | copy-start | bytes 1327108

commit v5 on v4

--- a/solution.py
+++ b/solution.py
@@ -33,7 +33,7 @@
     return (y >= 0) & (y < BY) & (x >= 0) & (x < BX)
 
 
-def kernel(x_in, w_in, g_in, out_ref, gi_ref, gw_ref,
+def kernel(x_in, w_in, g_in, out_ref, gw_ref,
            xf, wf, wt, mg, gip, gwp, yv, halo, r0, ra, rb, rg, sg, edge_s, edge_r, ssem, rsem):
     r = lax.axis_index("row")
     c = lax.axis_index("col")
@@ -395,14 +395,14 @@
     def step_o(z):
         edges[1 - z].wait_recv()
         gone = r == (NZ - 1 if z else 0)
-        out_ref[z] = (own[z] + jnp.where(gone, 0.0, edge_r[1 - z])).astype(bf16)
+        out_ref[z, 0:32] = (own[z] + jnp.where(gone, 0.0, edge_r[1 - z])).astype(bf16)
 
     ops = dict(s=step_s, t=step_t, y=step_y, p=step_p, o=step_o, g=gw_step, j=join,
                a=step_a2, b=step_b, c=step_b2, f=finish)
     for word in SCHED:
         ops[word[0]](int(word[1:]))
     for l in range(SLICES):
-        gi_ref[l * SL // N, :, l * SL % N:l * SL % N + SL] = gip[l, rows(mine + p * 128 + q * 32, 32, 32), :].astype(bf16)
+        out_ref[l * SL // N, 32:64, l * SL % N:l * SL % N + SL] = gip[l, rows(mine + p * 128 + q * 32, 32, 32), :].astype(bf16)
     gw_ref[...] = gwp[:, wcols(r)] * (1.0 / math.sqrt(16 * N))
     for copy in made:
         copy.wait_send()
@@ -413,13 +413,12 @@
     wr = weight.transpose(1, 0, 2).reshape(27 * 32, 128)
     gr = grad_out.transpose(1, 0, 2)
     vm = pl.BlockSpec(memory_space=pltpu.VMEM)
-    out, gi, gw = pl.pallas_call(
+    fields, gw = pl.pallas_call(
         kernel,
-        out_shape=(jax.ShapeDtypeStruct((2, 32, N), bf16),
-                   jax.ShapeDtypeStruct((2, 32, N), bf16),
+        out_shape=(jax.ShapeDtypeStruct((2, 64, N), bf16),
                    jax.ShapeDtypeStruct((864, 128), f32)),
         in_specs=[vm] * 3,
-        out_specs=(vm,) * 3,
+        out_specs=(vm,) * 2,
         scratch_shapes=[
             pltpu.VMEM((1024, 2 * N), bf16),
             pltpu.VMEM((864, 1024), bf16),
@@ -443,7 +442,8 @@
             collective_id=0, has_side_effects=True, vmem_limit_bytes=58 << 20),
         name="layer",
     )(xr, wr, gr)
-    return (out.transpose(1, 0, 2), gi.transpose(1, 0, 2),
+    fields = fields.transpose(1, 0, 2)
+    return (fields[:32], fields[32:],
             gw.reshape(27, 32, 128).transpose(1, 0, 2))
 
 

time: 79.4 us -> 78.6 us (0.990)
  local copies, waits for them, and re-layouts: 5.93 us -> 5.11 us
    unnamed x5, local copies, waits for them, and re-layouts: 4.21 us -> 2.35 us
    slice x0 -> x1, local copies, waits for them, and re-layouts: none -> 1.04 us  [on_device(): fields[32:]]
where the time goes in v5:
time: 78.6 us; the launch traced here: 77.4 us
  Pallas kernels  71.7 us (91%)
  local copies, waits for them, and re-layouts  5.11 us (7%)
    pallas_call x1, Pallas kernels, on_device(): pl.pallas_call(kernel, out_shape=(jax.ShapeDtypeStruct((2, 64, N), bf16),...  71.7 us
    unnamed x5, local copies, waits for them, and re-layouts  2.35 us
    transpose x1, local copies, waits for them, and re-layouts, on_device(): gr = grad_out.transpose(1, 0, 2)  1.72 us

profile of v5, /device:TPU:8, one launch (start us, length us, event | category | flops | bytes accessed | tf_op | source)
XLA Modules:
  0.0 77.4 jit_solution(12587695329246952809)
XLA Ops:
  0.6 1.7 %copy_bitcast_fusion = (bf16[2,32,1024]{2,1,0:T(8,128)(2,1)}, bf16[2,32,1024]{2,1,0:T(8,128)(2,1)}) fusion(bf16[32,2,1024]{2,1,0:T(2,128)(2,1)} %param.5, bf16[32,2,1024]{2,1,0:T(2,128)(2,1)} %param.3), kind=kLoop, calls=%fused_computation | loop fusion | bytes 524288 | tf_op jit(solution)/shard_map/transpose | solution.py:414
  2.4 71.7 %layer.1 = (bf16[2,64,1024]{2,1,0:T(8,128)(2,1)}, f32[864,128]{1,0:T(8,128)}) custom-call(bf16[2,32,1024]{2,1,0:T(8,128)(2,1)} %get-tuple-element.13.x_in, bf16[864,128]{1,0:T(8,128)(2,1)} %bitcast.13, bf16[2,32,1024]{2,1,0:T(8,128)(2,1)} %get-tuple-element.12.g_in), custom_call_target="tpu_custom_call" | custom-call | tf_op jit(solution)/shard_map/layer/pallas_call | solution.py:416
  74.0 0.0 copy-start
  74.1 1.0 %fusion = (bf16[32,2,1024]{2,0,1:T(8,128)(2,1)S(1)}, bf16[32,2,1024]{2,0,1:T(8,128)(2,1)S(1)}) fusion(bf16[64,2,1024]{2,0,1:T(8,128)(2,1)} %bitcast.12), kind=kLoop, calls=%fused_computation.2 | loop fusion | bytes 524288 | tf_op jit(solution)/shard_map/slice | solution.py:446
  75.1 0.8 %copy.9 = bf16[32,2,1024]{2,1,0:T(2,128)(2,1)} copy(bf16[32,2,1024]{2,0,1:T(8,128)(2,1)S(1)} %get-tuple-element.10) | data formatting | bytes 262144
  75.9 0.8 %copy.8 = bf16[32,2,1024]{2,1,0:T(2,128)(2,1)} copy(bf16[32,2,1024]{2,0,1:T(8,128)(2,1)S(1)} %get-tuple-element.11) | data formatting | bytes 262144
  76.7 0.0 copy-done
  76.7 0.8 copy.13
Async XLA Ops:
  74.0 2.6 %copy-start = (f32[864,128]{1,0:T(8,128)S(1)}, f32[864,128]{1,0:T(8,128)}, u32[]{:S(2)}) copy-start(f32[864,128]{1,0:T(8,128)} %get-tuple-element.6) | copy-start | bytes 1327108
